TPU v7x, 32 devices: a whole 2x2x4 slice. The times are simulated.
32 devices in a mesh: dp: 4 (over z), tensor: 8 (over y, x, core).
Axes of the slice: x: 2, y: 2, z: 4, core: 2. Of those that a mesh axis runs over, the one named last changes fastest.
Arguments:
- gradients: bfloat16 [4, 64, 512, 512], P('dp', None, 'tensor'), may hold values from -240 to 240
- momentum: bfloat16 [4, 32, 512, 512], P('dp', None, 'tensor'), may hold values from -36 to 36
- owners: int32 [64], replicated, may hold values from 0 to 3, as said below
Outputs:
- updates: float32 [4, 32, 512, 512], P('dp', None, 'tensor')
Inputs may be any that keep to these rules, and one draw needn't show every extreme that they name: `owners`: the blocks b with b // 16 == h give at most 8 blocks to any one owner, and exactly 8 to some owner, for every h; each owner holds at most 32 blocks, and some owner holds exactly 32.
All inputs are finite; a program needn't handle non-finite values.
Results may differ from a plain program's by a relative error of at most 0.018.
Values may be sent and summed in bfloat16 or wider, within the bound.
A program may use at most 64 MiB of HBM per device.

v0:
```python
import math

import jax
import jax.numpy as jnp
from jax import lax
from jax.sharding import PartitionSpec as P

ITERS = 3


decay_rate = 0.95
newton_a = 3.4445
newton_b = -4.775
newton_c = 2.0315
norm_eps = 1e-07


def ranks_of(labels):
    length = labels.shape[0]
    places = jnp.arange(length, dtype=jnp.int32)
    earlier = (labels[None, :] == labels[:, None]) & (places[None, :] < places[:, None])
    return jnp.sum(earlier.astype(jnp.int32), axis=1)


def iterate(blocks):
    widened = blocks.astype(jnp.float32)
    lengths = jnp.sqrt(jnp.sum(widened * widened, axis=(1, 2), keepdims=True)) + norm_eps
    current = widened / lengths
    scale_up = math.sqrt(blocks.shape[1])
    highest = lax.Precision.HIGHEST
    for iteration in range(ITERS):
        squared = jnp.einsum(
            "kij,klj->kil", current, current, precision=highest, preferred_element_type=jnp.float32
        )
        polynomial = newton_b * squared + newton_c * jnp.einsum(
            "kij,kjl->kil", squared, squared, precision=highest, preferred_element_type=jnp.float32
        )
        current = newton_a * current + jnp.einsum(
            "kij,kjl->kil",
            polynomial,
            current,
            precision=highest,
            preferred_element_type=jnp.float32,
        )
    return current * scale_up


def body(gradients, momentum, owners):
    dp_count = lax.axis_size("dp")
    tp_count = lax.axis_size("tensor")
    my_group = lax.axis_index("dp")
    pieces = gradients[0]
    blocks_all = pieces.shape[0]
    per_group = blocks_all // dp_count
    capacity = momentum.shape[1]
    places = jnp.arange(blocks_all, dtype=jnp.int32)
    slot_rank = ranks_of(owners)
    slot_ids = jnp.arange(capacity, dtype=jnp.int32)
    groups = jnp.arange(dp_count, dtype=jnp.int32)
    my_slots = (owners[:, None] == my_group) & (slot_rank[:, None] == slot_ids[None, :])
    occupied = jnp.any(my_slots, axis=0)
    held_sum = (
        lax.psum_scatter(pieces, "dp", scatter_dimension=0, tiled=True)
        .astype(jnp.float32)
        .astype(jnp.bfloat16)
    )
    pair_most = (2 * per_group + dp_count - 1) // dp_count
    held_owner = lax.dynamic_slice_in_dim(owners, my_group * per_group, per_group)
    held_rank = ranks_of(held_owner)
    held_places = jnp.arange(per_group, dtype=jnp.int32)
    pair_ids = jnp.arange(pair_most, dtype=jnp.int32)
    matched = (held_owner[:, None, None] == groups[None, :, None]) & (
        held_rank[:, None, None] == pair_ids[None, None, :]
    )
    source = jnp.sum(jnp.where(matched, held_places[:, None, None], 0), axis=0).reshape(-1)
    filled = jnp.any(matched, axis=0).reshape(-1)
    selected = jnp.take(held_sum, source, axis=0)
    outgoing = jnp.where(filled[:, None, None], selected, jnp.zeros_like(selected))
    outgoing = outgoing.reshape(dp_count, pair_most, pieces.shape[1], pieces.shape[2])
    incoming = lax.all_to_all(outgoing, "dp", split_axis=0, concat_axis=0, tiled=True)
    incoming = incoming.reshape(dp_count * pair_most, pieces.shape[1], pieces.shape[2])
    group_rank = ranks_of(owners * dp_count + places // per_group)
    position = places // per_group * pair_most + group_rank
    arriving = jnp.sum(jnp.where(my_slots, position[:, None], 0), axis=0)
    chosen = jnp.take(incoming, arriving, axis=0)
    gradient = jnp.where(occupied[:, None, None], chosen, jnp.zeros_like(chosen))
    widened_g = gradient.astype(jnp.float32)
    widened_m = momentum[0].astype(jnp.float32)
    blended = (widened_g + decay_rate * (decay_rate * widened_m + widened_g)).astype(jnp.bfloat16)
    per_device = (capacity + tp_count - 1) // tp_count
    total_slots = per_device * tp_count
    padded = jnp.pad(blended, ((0, total_slots - capacity), (0, 0), (0, 0)))
    padded = padded.reshape(tp_count, per_device, blended.shape[1], blended.shape[2])
    finished = iterate(
        lax.all_to_all(padded, "tensor", split_axis=0, concat_axis=2, tiled=True)[0]
    )[None]
    result = lax.all_to_all(
        finished.astype(jnp.bfloat16), "tensor", split_axis=2, concat_axis=0, tiled=True
    ).astype(finished.dtype)
    update = result.reshape(total_slots, blended.shape[1], blended.shape[2])[:capacity]
    update = jnp.where(occupied[:, None, None], update, jnp.zeros_like(update))
    return update[None]


def solution(mesh):
    in_specs = (P("dp", None, "tensor", None), P("dp", None, "tensor", None), P())
    out_specs = P("dp", None, "tensor", None)
    return jax.shard_map(body, mesh=mesh, in_specs=in_specs, out_specs=out_specs, check_vma=False)
```

profile of v0, /device:TPU:0, one launch (start us, length us, event | category | flops | bytes accessed | tf_op | source)
XLA Modules:
  0.0 296.1 jit_solution(16603282084117530750)
XLA Ops:
  6.5 0.7 reduce-scatter.2.cloned.1.call-update
  7.4 0.2 convert_reduce_fusion.2
  7.8 0.2 and_reduce_fusion
  8.0 81.2 %reduce-scatter.2.cloned.1.call-done = bf16[16,64,512]{2,1,0:T(8,128)(2,1)} async-done(((bf16[64,64,512]{2,1,0:T(8,128)(2,1)}), bf16[16,64,512]{2,1,0:T(8,128)(2,1)}) %reduce-scatter.2.cloned.1.call-update) | async-done | bytes 1048592 | tf_op jit(solution)/shard_map/reduce_scatter | solution.py:63
  89.2 1.9 gather_fusion
  91.1 1.7 select_select_fusion
  92.8 4.2 %all-to-all-start = ((bf16[4,8,64,512]{3,2,1,0:T(8,128)(2,1)}), bf16[4,8,64,512]{3,2,1,0:T(8,128)(2,1)S(1)}, u32[]{:S(2)}, u32[]{:S(2)}) async-start(bf16[4,8,64,512]{3,2,1,0:T(8,128)(2,1)} %select_select_fusion), calls=%async_computation.1 | async-start | bytes 4194304 | tf_op jit(solution)/shard_map/all_to_all | solution.py:80
  97.0 0.2 convert_reduce_fusion.1
  97.4 0.2 convert_reduce_fusion
  97.8 4.2 %convert_multiply_fusion.1 = f32[1,32,64,512]{3,2,1,0:T(8,128)} fusion(bf16[1,32,64,512]{3,2,1,0:T(8,128)(2,1)} %param.4), kind=kLoop, calls=%fused_computation.25 | loop fusion | flops 2097152 | bytes 6291456 | tf_op jit(solution)/shard_map/mul | solution.py:89
  102.1 43.0 %all-to-all-done = bf16[4,8,64,512]{3,2,1,0:T(8,128)(2,1)S(1)} async-done(((bf16[4,8,64,512]{3,2,1,0:T(8,128)(2,1)}), bf16[4,8,64,512]{3,2,1,0:T(8,128)(2,1)S(1)}, u32[]{:S(2)}, u32[]{:S(2)}) %all-to-all-start) | async-done | bytes 2097184 | tf_op jit(solution)/shard_map/all_to_all | solution.py:80
  145.1 1.3 copy-done
  146.5 2.3 gather_fusion.1
  148.7 3.5 %fusion.1 = bf16[8,4,64,512]{3,2,1,0:T(8,128)(2,1)S(1)} fusion(f32[8,4,64,512]{3,2,1,0:T(8,128)} %bitcast.35, bf16[8,4,64,512]{3,2,1,0:T(8,128)(2,1)S(1)} %bitcast.37, pred[8,4]{1,0:T(8,128)(4,1)S(1)} %compare_and_fusion, pred[8,4]{1,0:T(8,128)(4,1)S(1)} %broadcast_in_dim.97), kind=kLoop, calls=%fused_computation.7 | loop fusion | flops 7340032 | bytes 8388672 | tf_op jit(solution)/shard_map/convert_element_type | solution.py:89
  152.2 30.0 %all_to_all.23 = bf16[8,4,64,512]{3,2,1,0:T(8,128)(2,1)S(1)} all-to-all(bf16[8,4,64,512]{3,2,1,0:T(8,128)(2,1)S(1)} %fusion.1), channel_id=1, replica_groups=mesh['dp'=4,'tensor'=8] {'tensor'}, dimensions={0} | all-to-all | bytes 4194304 | tf_op jit(solution)/shard_map/all_to_all | solution.py:95
  182.3 0.6 fusion.2
  182.9 0.6 convert_bitcast_fusion
  183.5 0.5 copy.13
  184.0 7.6 %fusion.28 = f32[4,512,512]{2,1,0:T(8,128)S(1)} fusion(f32[4,512,512]{2,1,0:T(8,128)S(1)} %bitcast.42, f32[4]{0:T(128)S(1)} %sqrt_add_fusion), kind=kOutput, calls=%fused_computation.36 | convolution fusion | flops 6443499520 | bytes 8388624 | tf_op jit(solution)/shard_map/kij,klj->kil/dot_general | solution.py:32
  191.6 7.9 %fusion.43 = f32[4,512,512]{2,1,0:T(8,128)S(1)} fusion(f32[4,512,512]{2,1,0:T(8,128)S(1)} %fusion.28), kind=kOutput, calls=%fused_computation.78 | convolution fusion | flops 6442450944 | bytes 8388608 | tf_op jit(solution)/shard_map/kij,kjl->kil/dot_general | solution.py:35
  199.5 8.1 %multiply_add_fusion.1 = f32[4,512,512]{2,1,0:T(8,128)S(1)} fusion(f32[4,512,512]{2,1,0:T(8,128)S(1)} %fusion.43, f32[4,512,512]{2,1,0:T(8,128)S(1)} %fusion.28, f32[4,512,512]{2,1,0:T(8,128)S(1)} %bitcast.43, f32[4]{0:T(128)S(1)} %sqrt_add_fusion), kind=kOutput, calls=%fused_computation.24 | convolution fusion | flops 6449790976 | bytes 16777232 | tf_op jit(solution)/shard_map/kij,kjl->kil/dot_general | solution.py:38
  207.6 7.6 %fusion.44 = f32[4,512,512]{2,1,0:T(8,128)S(1)} fusion(f32[4,512,512]{2,1,0:T(8,128)S(1)} %multiply_add_fusion.1), kind=kOutput, calls=%fused_computation.79 | convolution fusion | flops 6442450944 | bytes 8388608 | tf_op jit(solution)/shard_map/kij,klj->kil/dot_general | solution.py:32
  215.2 7.4 %fusion.45 = f32[4,512,512]{2,1,0:T(8,128)S(1)} fusion(f32[4,512,512]{2,1,0:T(8,128)S(1)} %fusion.44), kind=kOutput, calls=%fused_computation.80 | convolution fusion | flops 6442450944 | bytes 8388608 | tf_op jit(solution)/shard_map/kij,kjl->kil/dot_general | solution.py:35
  222.6 8.0 %multiply_add_fusion = f32[4,512,512]{2,1,0:T(8,128)S(1)} fusion(f32[4,512,512]{2,1,0:T(8,128)S(1)} %multiply_add_fusion.1, f32[4,512,512]{2,1,0:T(8,128)S(1)} %fusion.45, f32[4,512,512]{2,1,0:T(8,128)S(1)} %fusion.44), kind=kOutput, calls=%fused_computation.19 | convolution fusion | flops 6447693824 | bytes 16777216 | tf_op jit(solution)/shard_map/kij,kjl->kil/dot_general | solution.py:38
  230.6 7.8 %fusion.46 = f32[4,512,512]{2,1,0:T(8,128)S(1)} fusion(f32[4,512,512]{2,1,0:T(8,128)S(1)} %multiply_add_fusion), kind=kOutput, calls=%fused_computation.81 | convolution fusion | flops 6442450944 | bytes 8388608 | tf_op jit(solution)/shard_map/kij,klj->kil/dot_general | solution.py:32
  238.4 7.4 %fusion.47 = f32[4,512,512]{2,1,0:T(8,128)S(1)} fusion(f32[4,512,512]{2,1,0:T(8,128)S(1)} %fusion.46), kind=kOutput, calls=%fused_computation.82 | convolution fusion | flops 6442450944 | bytes 8388608 | tf_op jit(solution)/shard_map/kij,kjl->kil/dot_general | solution.py:35
  245.8 7.9 %fusion.15 = bf16[1,4,512,512]{3,2,1,0:T(8,128)(2,1)S(1)} fusion(f32[4,512,512]{2,1,0:T(8,128)S(1)} %multiply_add_fusion, f32[4,512,512]{2,1,0:T(8,128)S(1)} %fusion.47, f32[4,512,512]{2,1,0:T(8,128)S(1)} %fusion.46), kind=kOutput, calls=%fused_computation.26 | convolution fusion | flops 6449790976 | bytes 14680064 | tf_op jit(solution)/shard_map/kij,kjl->kil/dot_general | solution.py:38
  253.7 1.6 copy.14
  255.4 29.0 %all_to_all.24 = bf16[1,4,512,512]{3,1,0,2:T(4,128)(2,1)S(1)} all-to-all(bf16[1,4,512,512]{3,1,0,2:T(4,128)(2,1)S(1)} %copy.14), channel_id=1, replica_groups=mesh['dp'=4,'tensor'=8] {'tensor'}, dimensions={2} | all-to-all | bytes 4194304 | tf_op jit(solution)/shard_map/all_to_all | solution.py:97
  284.4 0.6 convert_bitcast_fusion.1
  285.0 1.3 copy.15
  286.2 2.8 broadcast_select_fusion
  (23 shorter events, 0.8 us)
Async XLA Ops:
  6.5 0.7 copy-start.1
  6.5 82.6 %reduce-scatter.2.cloned.1.call-start = ((), (), s32[]{:S(2)}) async-start(), calls=%async_computation.4 | async-start | bytes 5242880 | tf_op jit(solution)/shard_map/reduce_scatter | solution.py:63
  92.8 52.3 %all-to-all-start = ((bf16[4,8,64,512]{3,2,1,0:T(8,128)(2,1)}), bf16[4,8,64,512]{3,2,1,0:T(8,128)(2,1)S(1)}, u32[]{:S(2)}, u32[]{:S(2)}) async-start(bf16[4,8,64,512]{3,2,1,0:T(8,128)(2,1)} %select_select_fusion), calls=%async_computation.1 | async-start | bytes 4194304 | tf_op jit(solution)/shard_map/all_to_all | solution.py:80
  145.1 1.4 copy-start
Sparse Core Ops, SparseCore 0:
  9.6 79.5 reduce-scatter.1
where the time goes:
time: 299 us; the launch traced here: 296 us
  waiting for transfers between devices  125 us (42%)
  matrix products  69.7 us (23%)
  blocking collectives  59 us (20%)
  other arithmetic  15.2 us (5%)
  between operations  13.8 us (5%)
  local copies, waits for them, and re-layouts  9.25 us (3%)
  starting transfers between devices  4.21 us (1%)
    reduce_scatter x1, waiting for transfers between devices, body(): lax.psum_scatter(pieces, 'dp', scatter_dimension=0, tiled=True)  81.2 us
    all_to_all x1, waiting for transfers between devices, body(): lax.all_to_all(outgoing, 'dp', split_axis=0, concat_axis=0, tiled=True)  43 us
    all_to_all x1, blocking collectives, body(): lax.all_to_all(padded, 'tensor', split_axis=0, concat_axis=2, tiled=True)[0]  30 us
    all_to_all x1, blocking collectives, body(): lax.all_to_all(finished.astype(jnp.bfloat16), 'tensor', split_axis=2, con...  29 us
    dot_general x3, matrix products, iterate(): jnp.einsum('kij,kjl->kil', polynomial, current, precision=highest, prefer...  24.1 us
    dot_general x3, matrix products, iterate(): jnp.einsum('kij,klj->kil', current, current, precision=highest, preferred...  22.9 us
    dot_general x3, matrix products, iterate(): jnp.einsum('kij,kjl->kil', squared, squared, precision=highest, preferred...  22.7 us
  transfers between devices with their start and end apart: 2, of which 2 were waited for; matrix products, arithmetic and copies ran while one was open for 2% of the time, Pallas kernels for 0%

commit v1 on v0

v1 whole, which is shorter than its diff:
```python
import math

import jax
import jax.numpy as jnp
from jax import lax
from jax.sharding import PartitionSpec as P

ITERS = 3


decay_rate = 0.95
newton_a = 3.4445
newton_b = -4.775
newton_c = 2.0315
norm_eps = 1e-07


def ranks_of(labels):
    length = labels.shape[0]
    places = jnp.arange(length, dtype=jnp.int32)
    earlier = (labels[None, :] == labels[:, None]) & (places[None, :] < places[:, None])
    return jnp.sum(earlier.astype(jnp.int32), axis=1)


def dot(spec, left, right):
    return jnp.einsum(
        spec,
        left.astype(jnp.bfloat16),
        right.astype(jnp.bfloat16),
        preferred_element_type=jnp.float32,
    )


def iterate(blocks):
    widened = blocks.astype(jnp.float32) * (1.0 + decay_rate)
    lengths = jnp.sqrt(jnp.sum(widened * widened, axis=(1, 2), keepdims=True)) + norm_eps
    current = widened / lengths
    scale_up = math.sqrt(blocks.shape[1])
    for iteration in range(ITERS):
        squared = dot("kij,klj->kil", current, current)
        polynomial = newton_b * squared + newton_c * dot("kij,kjl->kil", squared, squared)
        current = newton_a * current + dot("kij,kjl->kil", polynomial, current)
    return current * scale_up


def body(gradients, momentum, owners):
    dp_count = lax.axis_size("dp")
    tp_count = lax.axis_size("tensor")
    my_group = lax.axis_index("dp")
    pieces = gradients[0]
    blocks_all, rows, columns = pieces.shape
    per_group = blocks_all // dp_count
    capacity = momentum.shape[1]
    slot_rank = ranks_of(owners)
    places = jnp.arange(blocks_all, dtype=jnp.int32)

    mine = owners == my_group
    moment = jnp.take(momentum[0], jnp.minimum(slot_rank, capacity - 1), axis=0)
    moment = jnp.where(mine[:, None, None], moment, jnp.zeros_like(moment)).astype(jnp.float32)
    ratio = decay_rate * decay_rate / (1.0 + decay_rate)
    folded = (pieces.astype(jnp.float32) + ratio * moment).astype(jnp.bfloat16)
    held = lax.psum_scatter(folded, "dp", scatter_dimension=0, tiled=True)

    per_device = (per_group + tp_count - 1) // tp_count
    padded_count = per_device * tp_count
    padded = jnp.pad(held, ((0, padded_count - per_group), (0, 0), (0, 0)))
    whole = lax.all_to_all(padded, "tensor", split_axis=0, concat_axis=1, tiled=True)
    finished = iterate(whole).astype(jnp.bfloat16)
    result = lax.all_to_all(finished, "tensor", split_axis=1, concat_axis=0, tiled=True)

    groups = jnp.arange(dp_count, dtype=jnp.int32)
    pair_most = (2 * per_group + dp_count - 1) // dp_count
    held_owner = lax.dynamic_slice_in_dim(owners, my_group * per_group, per_group)
    held_rank = ranks_of(held_owner)
    held_places = jnp.arange(per_group, dtype=jnp.int32)
    pair_ids = jnp.arange(pair_most, dtype=jnp.int32)
    matched = (held_owner[:, None, None] == groups[None, :, None]) & (
        held_rank[:, None, None] == pair_ids[None, None, :]
    )
    source = jnp.sum(jnp.where(matched, held_places[:, None, None], 0), axis=0).reshape(-1)
    outgoing = jnp.take(result, source, axis=0)
    outgoing = outgoing.reshape(dp_count, pair_most, rows, columns)
    incoming = lax.all_to_all(outgoing, "dp", split_axis=0, concat_axis=0, tiled=True)
    incoming = incoming.reshape(dp_count * pair_most, rows, columns)
    group_rank = ranks_of(owners * dp_count + places // per_group)
    position = places // per_group * pair_most + group_rank
    slot_ids = jnp.arange(capacity, dtype=jnp.int32)
    my_slots = mine[:, None] & (slot_rank[:, None] == slot_ids[None, :])
    occupied = jnp.any(my_slots, axis=0)
    arriving = jnp.sum(jnp.where(my_slots, position[:, None], 0), axis=0)
    chosen = jnp.take(incoming, arriving, axis=0).astype(jnp.float32)
    update = jnp.where(occupied[:, None, None], chosen, jnp.zeros_like(chosen))
    return update[None]


def solution(mesh):
    in_specs = (P("dp", None, "tensor", None), P("dp", None, "tensor", None), P())
    out_specs = P("dp", None, "tensor", None)
    return jax.shard_map(body, mesh=mesh, in_specs=in_specs, out_specs=out_specs, check_vma=False)
```

time: 299 us -> 241 us (0.81)
  blocking collectives: 59 us -> 0 us
  matrix products: 69.7 us -> 29.6 us
  waiting for transfers between devices: 125 us -> 155 us
  starting transfers between devices: 4.21 us -> 11.7 us
  local copies, waits for them, and re-layouts: 9.25 us -> 12.4 us
    all_to_all x2 -> x0, blocking collectives: 59 us -> none  [the longest x1 30 us: body(): lax.all_to_all(padded, 'tensor', split_axis=0, concat_axis=2, tiled=True)[0]]
    dot_general x9 -> x6, matrix products: 69.7 us -> 29.6 us  [dot(): jnp.einsum(spec, left.astype(jnp.bfloat16), right.astype(jnp.bfloat16), p...]
    all_to_all x0 -> x2, waiting for transfers between devices: none -> 30.1 us  [the longest x1 15.3 us: body(): lax.all_to_all(padded, 'tensor', split_axis=0, concat_axis=1, tiled=True)]
    all_to_all x0 -> x2, starting transfers between devices: none -> 7.22 us  [the longest x1 3.66 us: body(): lax.all_to_all(padded, 'tensor', split_axis=0, concat_axis=1, tiled=True)]
    gather x2 -> x3, local copies, waits for them, and re-layouts: 4.17 us -> 8.39 us  [the longest x1 3.56 us: body(): chosen = jnp.take(incoming, arriving, axis=0).astype(jnp.float32)]
    mul x1, other arithmetic: 4.22 us -> 0.31 us  [iterate(): widened = blocks.astype(jnp.float32) * (1.0 + decay_rate)]
    select_n x4 -> x5, other arithmetic: 4.48 us -> 7.81 us  [the longest x1 4.63 us: body(): update = jnp.where(occupied[:, None, None], chosen, jnp.zeros_like(chosen))]
    convert_element_type x3 -> x1, other arithmetic: 4.65 us -> 6.45 us  [body(): folded = (pieces.astype(jnp.float32) + ratio * moment).astype(jnp.bfloat16)]
  transfers between devices with their start and end apart: 2 -> 4, of which waited for: 2 -> 4; matrix products, arithmetic and copies ran while one was open for 2% -> 0% of each run, Pallas kernels for 0% -> 0%
where the time goes in v1:
time: 241 us; the launch traced here: 240 us
  waiting for transfers between devices  155 us (64%)
  matrix products  29.6 us (12%)
  other arithmetic  17.8 us (7%)
  between operations  13.6 us (6%)
  local copies, waits for them, and re-layouts  12.4 us (5%)
  starting transfers between devices  11.7 us (5%)
    reduce_scatter x1, waiting for transfers between devices, body(): held = lax.psum_scatter(folded, 'dp', scatter_dimension=0, tiled=True)  79.7 us
    all_to_all x1, waiting for transfers between devices, body(): lax.all_to_all(outgoing, 'dp', split_axis=0, concat_axis=0, tiled=True)  45.6 us
    dot_general x6, matrix products, dot(): jnp.einsum(spec, left.astype(jnp.bfloat16), right.astype(jnp.bfloat16), p...  29.6 us
    all_to_all x1, waiting for transfers between devices, body(): lax.all_to_all(padded, 'tensor', split_axis=0, concat_axis=1, tiled=True)  15.3 us
    all_to_all x1, waiting for transfers between devices, body(): lax.all_to_all(finished, 'tensor', split_axis=1, concat_axis=0, tiled=True)  14.8 us
    convert_element_type x1, other arithmetic, body(): folded = (pieces.astype(jnp.float32) + ratio * moment).astype(jnp.bfloat16)  6.45 us
  transfers between devices with their start and end apart: 4, of which 4 were waited for; matrix products, arithmetic and copies ran while one was open for 0% of the time, Pallas kernels for 0%

profile of v1, /device:TPU:0, one launch (start us, length us, event | category | flops | bytes accessed | tf_op | source)
XLA Modules:
  0.0 240.3 jit_solution(11700916284056915022)
XLA Ops:
  6.5 1.0 convert_reduce_fusion.1
  7.6 0.7 compare_and_fusion
  8.2 2.8 %gather_fusion = bf16[64,64,512]{2,1,0:T(8,128)(2,1)} fusion(bf16[32,64,512]{2,1,0:T(8,128)(2,1)S(1)} %bitcast.29, s32[1024]{0:T(1024)S(1)} %pad_clamp_fusion.2), kind=kCustom, calls=%fused_computation | custom fusion | bytes 8388864 | tf_op jit(solution)/shard_map/jit(_take)/gather | solution.py:58
  11.1 6.5 %fusion = bf16[64,64,512]{2,1,0:T(8,128)(2,1)} fusion(bf16[1,64,64,512]{3,2,1,0:T(8,128)(2,1)} %param.3, bf16[64,64,512]{2,1,0:T(8,128)(2,1)} %gather_fusion, pred[64]{0:T(512)(128)(4,1)S(1)} %get-tuple-element.5, pred[64]{0:T(512)(128)(4,1)S(1)} %get-tuple-element.6), kind=kLoop, calls=%fused_computation.4 | loop fusion | flops 14680064 | bytes 12583040 | tf_op jit(solution)/shard_map/convert_element_type | solution.py:61
  17.6 79.7 %reduce-scatter.2.cloned.1.call-done = bf16[16,64,512]{2,1,0:T(8,128)(2,1)} async-done(((bf16[64,64,512]{2,1,0:T(8,128)(2,1)}), bf16[16,64,512]{2,1,0:T(8,128)(2,1)}) %reduce-scatter.2.cloned.1.call-update) | async-done | bytes 1048592 | tf_op jit(solution)/shard_map/reduce_scatter | solution.py:62
  97.2 3.7 %all-to-all-start = ((bf16[16,64,512]{2,1,0:T(8,128)(2,1)}), bf16[16,64,512]{2,1,0:T(8,128)(2,1)S(1)}, u32[]{:S(2)}, u32[]{:S(2)}) async-start(bf16[16,64,512]{2,1,0:T(8,128)(2,1)} %reduce-scatter.2.cloned.1.call-done), calls=%async_computation.1 | async-start | bytes 2097152 | tf_op jit(solution)/shard_map/all_to_all | solution.py:67
  101.0 15.3 %all-to-all-done = bf16[16,64,512]{2,1,0:T(8,128)(2,1)S(1)} async-done(((bf16[16,64,512]{2,1,0:T(8,128)(2,1)}), bf16[16,64,512]{2,1,0:T(8,128)(2,1)S(1)}, u32[]{:S(2)}, u32[]{:S(2)}) %all-to-all-start) | async-done | bytes 1048608 | tf_op jit(solution)/shard_map/all_to_all | solution.py:67
  116.3 0.3 convert_multiply_fusion
  116.6 0.2 copy.13
  116.8 0.4 multiply_reduce_fusion
  117.2 0.3 bitcast_divide_fusion
  117.6 1.3 copy-done.1
  118.9 2.0 fusion.20
  120.9 6.8 %multiply_add_fusion.1 = f32[2,512,512]{2,1,0:T(8,128)} fusion(f32[2,512,512]{2,1,0:T(8,128)} %copy-done.1, f32[2,512,512]{2,1,0:T(8,128)} %fusion.20), kind=kOutput, calls=%fused_computation.13 | convolution fusion | flops 1077936128 | bytes 6291456 | tf_op jit(solution)/shard_map/kij,kjl->kil/dot_general | solution.py:26
  127.7 4.3 %fusion.17 = f32[2,512,512]{2,1,0:T(8,128)} fusion(f32[2,512,512]{2,1,0:T(8,128)} %multiply_add_fusion.1), kind=kOutput, calls=%fused_computation.30 | convolution fusion | flops 537395200 | bytes 4194304 | tf_op jit(solution)/shard_map/kij,klj->kil/dot_general | solution.py:26
  132.0 6.7 %multiply_add_fusion = f32[2,512,512]{2,1,0:T(8,128)} fusion(f32[2,512,512]{2,1,0:T(8,128)} %multiply_add_fusion.1, f32[2,512,512]{2,1,0:T(8,128)} %fusion.17), kind=kOutput, calls=%fused_computation.11 | convolution fusion | flops 1077936128 | bytes 6291456 | tf_op jit(solution)/shard_map/kij,kjl->kil/dot_general | solution.py:26
  138.7 4.3 %fusion.14 = f32[2,512,512]{2,1,0:T(8,128)} fusion(f32[2,512,512]{2,1,0:T(8,128)} %multiply_add_fusion), kind=kOutput, calls=%fused_computation.27 | convolution fusion | flops 537395200 | bytes 4194304 | tf_op jit(solution)/shard_map/kij,klj->kil/dot_general | solution.py:26
  143.0 5.5 %multiply_convert_fusion = bf16[2,512,512]{2,1,0:T(8,128)(2,1)S(1)} fusion(f32[2,512,512]{2,1,0:T(8,128)} %multiply_add_fusion, f32[2,512,512]{2,1,0:T(8,128)} %fusion.14), kind=kOutput, calls=%fused_computation.8 | convolution fusion | flops 1078984704 | bytes 5242880 | tf_op jit(solution)/shard_map/kij,kjl->kil/dot_general | solution.py:26
  148.5 2.0 copy.14
  150.5 3.6 %all-to-all-start.1 = ((bf16[2,512,512]{2,0,1:T(2,128)(2,1)}), bf16[2,512,512]{2,0,1:T(2,128)(2,1)S(1)}, u32[]{:S(2)}, u32[]{:S(2)}) async-start(bf16[2,512,512]{2,0,1:T(2,128)(2,1)} %copy.14), calls=%async_computation.2 | async-start | bytes 2097152 | tf_op jit(solution)/shard_map/all_to_all | solution.py:69
  154.1 0.2 convert_reduce_fusion.2
  154.3 0.2 select_reduce_fusion
  154.5 14.8 %all-to-all-done.1 = bf16[2,512,512]{2,0,1:T(2,128)(2,1)S(1)} async-done(((bf16[2,512,512]{2,0,1:T(2,128)(2,1)}), bf16[2,512,512]{2,0,1:T(2,128)(2,1)S(1)}, u32[]{:S(2)}, u32[]{:S(2)}) %all-to-all-start.1) | async-done | bytes 1048608 | tf_op jit(solution)/shard_map/all_to_all | solution.py:69
  169.4 0.2 copy.15
  169.6 2.0 gather_fusion.1
  171.6 3.2 %broadcast_select_fusion = bf16[4,8,64,512]{3,2,1,0:T(8,128)(2,1)} fusion(bf16[4,8,64,512]{3,2,1,0:T(8,128)(2,1)} %bitcast.33, pred[4,8]{1,0:T(4,128)(4,1)S(1)} %compare_and_fusion.1), kind=kLoop, calls=%fused_computation.16 | loop fusion | flops 1048576 | bytes 4194336 | tf_op jit(solution)/shard_map/jit(_take)/select_n | solution.py:81
  174.8 4.4 %all-to-all-start.2 = ((bf16[4,8,64,512]{3,2,1,0:T(8,128)(2,1)}), bf16[4,8,64,512]{3,2,1,0:T(8,128)(2,1)}, u32[]{:S(2)}, u32[]{:S(2)}) async-start(bf16[4,8,64,512]{3,2,1,0:T(8,128)(2,1)} %broadcast_select_fusion), calls=%async_computation.3 | async-start | bytes 4194304 | tf_op jit(solution)/shard_map/all_to_all | solution.py:83
  179.3 0.2 convert_reduce_fusion
  179.6 0.1 fusion.25
  179.7 45.6 %all-to-all-done.2 = bf16[4,8,64,512]{3,2,1,0:T(8,128)(2,1)} async-done(((bf16[4,8,64,512]{3,2,1,0:T(8,128)(2,1)}), bf16[4,8,64,512]{3,2,1,0:T(8,128)(2,1)}, u32[]{:S(2)}, u32[]{:S(2)}) %all-to-all-start.2) | async-done | bytes 2097184 | tf_op jit(solution)/shard_map/all_to_all | solution.py:83
  225.3 3.6 %gather_fusion.2 = bf16[32,64,512]{2,1,0:T(8,128)(2,1)} fusion(bf16[32,64,512]{2,1,0:T(8,128)(2,1)} %bitcast.12, s32[1024]{0:T(1024)S(1)} %pad_clamp_fusion), kind=kCustom, calls=%fused_computation.2 | custom fusion | bytes 4194432 | tf_op jit(solution)/shard_map/jit(_take)/gather | solution.py:91
  228.8 4.6 %convert_select_fusion = f32[1,32,64,512]{3,2,1,0:T(8,128)} fusion(bf16[32,64,512]{2,1,0:T(8,128)(2,1)} %gather_fusion.2, pred[32]{0:T(512)(128)(4,1)S(1)} %compare_and_fusion.2, pred[32]{0:T(512)(128)(4,1)S(1)} %fusion.25), kind=kLoop, calls=%fused_computation.5 | loop fusion | flops 3145728 | bytes 6291520 | tf_op jit(solution)/shard_map/jit(_where)/select_n | solution.py:92
  (24 shorter events, 0.5 us)
Async XLA Ops:
  6.5 1.7 copy-start
  6.5 90.7 %reduce-scatter.2.cloned.1.call-start = ((), (), s32[]{:S(2)}) async-start(), calls=%async_computation.4 | async-start | bytes 5242880 | tf_op jit(solution)/shard_map/reduce_scatter | solution.py:62
  17.5 83.3 %copy-start.2 = (s32[64]{0:T(128)S(1)}, s32[64]{0:T(128)}, u32[]{:S(2)}) copy-start(s32[64]{0:T(128)} %param.5) | copy-start | bytes 772
  97.2 19.0 %all-to-all-start = ((bf16[16,64,512]{2,1,0:T(8,128)(2,1)}), bf16[16,64,512]{2,1,0:T(8,128)(2,1)S(1)}, u32[]{:S(2)}, u32[]{:S(2)}) async-start(bf16[16,64,512]{2,1,0:T(8,128)(2,1)} %reduce-scatter.2.cloned.1.call-done), calls=%async_computation.1 | async-start | bytes 2097152 | tf_op jit(solution)/shard_map/all_to_all | solution.py:67
  117.5 1.3 copy-start.1
  150.5 18.9 %all-to-all-start.1 = ((bf16[2,512,512]{2,0,1:T(2,128)(2,1)}), bf16[2,512,512]{2,0,1:T(2,128)(2,1)S(1)}, u32[]{:S(2)}, u32[]{:S(2)}) async-start(bf16[2,512,512]{2,0,1:T(2,128)(2,1)} %copy.14), calls=%async_computation.2 | async-start | bytes 2097152 | tf_op jit(solution)/shard_map/all_to_all | solution.py:69
  174.8 50.5 %all-to-all-start.2 = ((bf16[4,8,64,512]{3,2,1,0:T(8,128)(2,1)}), bf16[4,8,64,512]{3,2,1,0:T(8,128)(2,1)}, u32[]{:S(2)}, u32[]{:S(2)}) async-start(bf16[4,8,64,512]{3,2,1,0:T(8,128)(2,1)} %broadcast_select_fusion), calls=%async_computation.3 | async-start | bytes 4194304 | tf_op jit(solution)/shard_map/all_to_all | solution.py:83
Sparse Core Ops, SparseCore 0:
  17.7 79.5 reduce-scatter.1

commit v2 on v1

--- a/solution.py
+++ b/solution.py
@@ -1,8 +1,11 @@
+import functools
 import math
 
 import jax
 import jax.numpy as jnp
 from jax import lax
+from jax.experimental import pallas as pl
+from jax.experimental.pallas import tpu as pltpu
 from jax.sharding import PartitionSpec as P
 
 ITERS = 3
@@ -93,7 +96,329 @@
     return update[None]
 
 
+MESH = pl.DeviceIdType.MESH
+
+
+def kernel(
+    sizes, weight, slot, g_ref, m_ref, out_ref,
+    arrived, partial, whole, ready, gathered, current,
+    chain_send, chain_recv, scatter_send, scatter_recv, return_send, ahead_send, gather_recv, out_sem,
+):
+    n, width, half, rows, lead = sizes
+    columns = g_ref.shape[2]
+    z, t = lax.axis_index("dp"), lax.axis_index("tensor")
+    per_device = half // width
+    is_end = (z == 0) | (z == n - 1)
+    low = 2 * z < n - 1
+
+    barrier = pltpu.get_barrier_semaphore()
+
+    @pl.when(z > 0)
+    def _():
+        pl.semaphore_signal(barrier, inc=1, device_id=(z - 1, t), device_id_type=MESH)
+
+    @pl.when(z < n - 1)
+    def _():
+        pl.semaphore_signal(barrier, inc=1, device_id=(z + 1, t), device_id_type=MESH)
+
+    def greet(k, carry):
+        peer = lax.rem(t + k, width)
+        pl.semaphore_signal(barrier, inc=1, device_id=(z, peer), device_id_type=MESH)
+        return carry
+
+    lax.fori_loop(1, width, greet, 0)
+    pl.semaphore_wait(barrier, jnp.where(is_end, width, width + 1))
+
+    def chain_copy(d, c):
+        return pltpu.make_async_remote_copy(
+            src_ref=partial.at[d, c],
+            dst_ref=arrived.at[d, c],
+            send_sem=chain_send.at[d, c],
+            recv_sem=chain_recv.at[d, c],
+            device_id=(z + 2 * d - 1, t),
+            device_id_type=MESH,
+        )
+
+    def own(d, c):
+        block = d * half + c
+        moment = m_ref[slot[block]].astype(jnp.float32)
+        return g_ref[block].astype(jnp.float32) + weight[block] * moment
+
+    def my_rows(place):
+        return pl.ds(pl.multiple_of(place * rows, rows), rows)
+
+    def start_chain(d, c):
+        partial[d, c] = own(d, c).astype(jnp.bfloat16)
+        chain_copy(d, c).start()
+
+    def add_chain(d, c):
+        chain_copy(d, c).wait_recv()
+        total = own(d, c) + arrived[d, c].astype(jnp.float32)
+        partial[d, c] = total.astype(jnp.bfloat16)
+
+    def scatter_copy(d, c, peer, sem):
+        return pltpu.make_async_remote_copy(
+            src_ref=partial.at[d, c],
+            dst_ref=whole.at[c // width, my_rows(t)],
+            send_sem=scatter_send.at[c],
+            recv_sem=sem,
+            device_id=(z, peer),
+            device_id_type=MESH,
+        )
+
+    def return_copy(d, j, peer):
+        block = d * half + j * width + t
+        return pltpu.make_async_remote_copy(
+            src_ref=ready.at[j, my_rows(peer)],
+            dst_ref=gathered.at[block],
+            send_sem=return_send.at[j, peer],
+            recv_sem=gather_recv.at[block],
+            device_id=(z, peer),
+            device_id_type=MESH,
+        )
+
+    def ahead_copy(d, c):
+        block = d * half + c
+        return pltpu.make_async_remote_copy(
+            src_ref=gathered.at[block],
+            dst_ref=gathered.at[block],
+            send_sem=ahead_send.at[block],
+            recv_sem=gather_recv.at[block],
+            device_id=(z + 1 - 2 * d, t),
+            device_id_type=MESH,
+        )
+
+    def iterate_in(j):
+        widened = whole[j].astype(jnp.float32) * (1.0 + decay_rate)
+        length = jnp.sqrt(jnp.sum(widened * widened)) + norm_eps
+        current[...] = widened / length
+
+        def once(k, carry):
+            now = current[...]
+            low_now = now.astype(jnp.bfloat16)
+            squared = lax.dot_general(
+                low_now, low_now, (((1,), (1,)), ((), ())), preferred_element_type=jnp.float32
+            )
+            low_squared = squared.astype(jnp.bfloat16)
+            polynomial = newton_b * squared + newton_c * jnp.dot(
+                low_squared, low_squared, preferred_element_type=jnp.float32
+            )
+            current[...] = newton_a * now + jnp.dot(
+                polynomial.astype(jnp.bfloat16), low_now, preferred_element_type=jnp.float32
+            )
+            return carry
+
+        lax.fori_loop(0, ITERS, once, 0)
+        ready[j] = (current[...] * math.sqrt(columns)).astype(jnp.bfloat16)
+
+    @pl.when(is_end)
+    def _():
+        near = jnp.where(z == 0, 0, 1)
+        far = 1 - near
+
+        def begin(c, carry):
+            start_chain(far, c)
+            return carry
+
+        lax.fori_loop(0, half, begin, 0)
+
+        def block_step(j, carry):
+            def chunk(k, inner):
+                c = j * width + k
+                add_chain(near, c)
+
+                @pl.when(k == t)
+                def _():
+                    pltpu.make_async_copy(
+                        partial.at[near, c], whole.at[j, my_rows(t)], scatter_recv.at[j, t]
+                    ).start()
+
+                @pl.when(k != t)
+                def _():
+                    scatter_copy(near, c, k, scatter_recv.at[j, t]).start()
+
+                return inner
+
+            lax.fori_loop(0, width, chunk, 0)
+
+            def land(k, inner):
+                pltpu.make_async_copy(
+                    partial.at[near, 0], whole.at[j, my_rows(k)], scatter_recv.at[j, k]
+                ).wait()
+                return inner
+
+            lax.fori_loop(0, width, land, 0)
+            iterate_in(j)
+
+            def give(k, inner):
+                @pl.when(k == t)
+                def _():
+                    block = near * half + j * width + t
+                    pltpu.make_async_copy(
+                        ready.at[j, my_rows(t)], gathered.at[block], gather_recv.at[block]
+                    ).start()
+
+                @pl.when(k != t)
+                def _():
+                    return_copy(near, j, k).start()
+
+                return inner
+
+            lax.fori_loop(0, width, give, 0)
+            return carry
+
+        lax.fori_loop(0, per_device, block_step, 0)
+
+    @pl.when(jnp.logical_not(is_end))
+    def _():
+        early = jnp.where(low, 1, 0)
+
+        def forward(d, c):
+            add_chain(d, c)
+            chain_copy(d, c).start()
+
+        def step(i, carry):
+            @pl.when(i < half)
+            def _():
+                forward(early, i)
+
+            @pl.when(i >= lead)
+            def _():
+                forward(1 - early, i - lead)
+
+            return carry
+
+        lax.fori_loop(0, half + lead, step, 0)
+
+    def pass_on(d, c):
+        ahead_copy(d, c).wait_recv()
+
+        @pl.when((z + 1 - 2 * d >= 0) & (z + 1 - 2 * d < n))
+        def _():
+            ahead_copy(d, c).start()
+
+    first = jnp.where(low, 0, 1)
+    delay = jnp.where(is_end, half, lead)
+
+    def gather_step(i, carry):
+        @pl.when(i < half)
+        def _():
+            pass_on(first, i)
+
+        @pl.when(i >= delay)
+        def _():
+            pass_on(1 - first, i - delay)
+
+        return carry
+
+    lax.fori_loop(0, half + delay, gather_step, 0)
+    final = pltpu.make_async_copy(gathered, out_ref, out_sem)
+    final.start()
+
+    for d in range(2):
+        sink = 0 if d == 0 else n - 1
+
+        def settle(c, carry):
+            @pl.when(z != sink)
+            def _():
+                chain_copy(d, c).wait_send()
+
+            @pl.when(z != n - 1 - sink)
+            def _():
+                ahead_copy(d, c).wait_send()
+
+            @pl.when((z == sink) & (lax.rem(c, width) != t))
+            def _():
+                scatter_copy(d, c, lax.rem(c, width), scatter_recv.at[0, 0]).wait_send()
+                return_copy(d, c // width, lax.rem(c, width)).wait_send()
+
+            return carry
+
+        lax.fori_loop(0, half, settle, 0)
+    final.wait()
+
+
+def pick_kernel(index, filled, in_ref, out_ref):
+    place = pl.program_id(0)
+    piece = in_ref[0].astype(jnp.float32)
+    out_ref[0, 0] = jnp.where(filled[place] > 0, piece, jnp.zeros_like(piece))
+
+
+def fused(gradients, momentum, owners):
+    n = lax.axis_size("dp")
+    width = lax.axis_size("tensor")
+    me = lax.axis_index("dp")
+    pieces = gradients[0]
+    blocks_all, rows, columns = pieces.shape
+    capacity = momentum.shape[1]
+    half = blocks_all // 2
+    lead = min(4, half)
+    slot_rank = ranks_of(owners)
+    mine = owners == me
+    ratio = decay_rate * decay_rate / (1.0 + decay_rate)
+    weight = jnp.where(mine, ratio, 0.0).astype(jnp.float32)
+    slot = jnp.minimum(slot_rank, capacity - 1)
+    order = columns
+    low = jnp.bfloat16
+    all_results = pl.pallas_call(
+        functools.partial(kernel, (n, width, half, rows, lead)),
+        out_shape=jax.ShapeDtypeStruct((blocks_all, rows, columns), low),
+        in_specs=[
+            pl.BlockSpec(memory_space=pltpu.SMEM),
+            pl.BlockSpec(memory_space=pltpu.SMEM),
+            pl.BlockSpec(memory_space=pltpu.VMEM),
+            pl.BlockSpec(memory_space=pltpu.VMEM),
+        ],
+        out_specs=pl.BlockSpec(memory_space=pl.ANY),
+        scratch_shapes=[
+            pltpu.VMEM((2, half, rows, columns), low),
+            pltpu.VMEM((2, half, rows, columns), low),
+            pltpu.VMEM((half // width, order, columns), low),
+            pltpu.VMEM((half // width, order, columns), low),
+            pltpu.VMEM((blocks_all, rows, columns), low),
+            pltpu.VMEM((order, columns), jnp.float32),
+            pltpu.SemaphoreType.DMA((2, half)),
+            pltpu.SemaphoreType.DMA((2, half)),
+            pltpu.SemaphoreType.DMA((half,)),
+            pltpu.SemaphoreType.DMA((half // width, width)),
+            pltpu.SemaphoreType.DMA((half // width, width)),
+            pltpu.SemaphoreType.DMA((blocks_all,)),
+            pltpu.SemaphoreType.DMA((blocks_all,)),
+            pltpu.SemaphoreType.DMA,
+        ],
+        compiler_params=pltpu.CompilerParams(
+            collective_id=0, has_side_effects=True, vmem_limit_bytes=50 * 1024 * 1024
+        ),
+        name="muon_chain",
+    )(weight, slot, pieces, momentum[0])
+
+    slot_ids = jnp.arange(capacity, dtype=jnp.int32)
+    places = jnp.arange(blocks_all, dtype=jnp.int32)
+    my_slots = mine[:, None] & (slot_rank[:, None] == slot_ids[None, :])
+    filled = jnp.any(my_slots, axis=0).astype(jnp.int32)
+    index = jnp.sum(jnp.where(my_slots, places[:, None], 0), axis=0)
+    return pl.pallas_call(
+        pick_kernel,
+        out_shape=jax.ShapeDtypeStruct((1, capacity, rows, columns), jnp.float32),
+        grid_spec=pltpu.PrefetchScalarGridSpec(
+            num_scalar_prefetch=2,
+            grid=(capacity,),
+            in_specs=[pl.BlockSpec((1, rows, columns), lambda s, index, filled: (index[s], 0, 0))],
+            out_specs=pl.BlockSpec((1, 1, rows, columns), lambda s, index, filled: (0, s, 0, 0)),
+        ),
+        name="muon_pick",
+    )(index, filled, all_results)
+
+
+def choose(gradients, momentum, owners):
+    n, width = lax.axis_size("dp"), lax.axis_size("tensor")
+    blocks_all = gradients.shape[1]
+    if n > 1 and blocks_all % (2 * width) == 0 and gradients.shape[2] % 16 == 0:
+        return fused(gradients, momentum, owners)
+    return body(gradients, momentum, owners)
+
+
 def solution(mesh):
     in_specs = (P("dp", None, "tensor", None), P("dp", None, "tensor", None), P())
     out_specs = P("dp", None, "tensor", None)
-    return jax.shard_map(body, mesh=mesh, in_specs=in_specs, out_specs=out_specs, check_vma=False)
+    return jax.shard_map(choose, mesh=mesh, in_specs=in_specs, out_specs=out_specs, check_vma=False)

time: 241 us -> 170 us (0.71)
  the two profiles are of different devices: /device:TPU:0 before, /device:TPU:28 now
where the time goes in v2:
time: 170 us; the launch traced here: 169 us
  Pallas kernels  164 us (96%)
  other arithmetic  2.88 us (2%)
    pallas_call x1, Pallas kernels, fused(): pl.pallas_call(functools.partial(kernel, (n, width, half, rows, lead)), o...  146 us
    pallas_call x1, Pallas kernels, fused(): pl.pallas_call(pick_kernel, out_shape=jax.ShapeDtypeStruct((1, capacity,...  17.7 us

profile of v2, /device:TPU:28, one launch (start us, length us, event | category | flops | bytes accessed | tf_op | source)
XLA Modules:
  0.0 168.5 jit_solution(7189712587257792692)
XLA Ops:
  0.0 0.9 convert_reduce_fusion
  0.9 0.7 broadcast_select_fusion
  1.6 0.1 fusion.2
  1.7 0.6 select_reduce_fusion.index
  2.3 0.5 convert_element_type.7.filled
  2.9 0.0 copy-start
  2.9 1.6 copy-done
  4.5 146.3 %muon_chain.1.in_ref = bf16[64,64,512]{2,1,0:T(8,128)(2,1)} custom-call(f32[64]{0:T(128)S(1)} %get-tuple-element.5.weight, s32[64]{0:T(128)S(1)} %broadcast_minimum_fusion.slot, bf16[64,64,512]{2,1,0:T(8,128)(2,1)} %bitcast.3, bf16[32,64,512]{2,1,0:T(8,128)(2,1)S(1)} %bitcast.2), custom_call_target="tpu_custom_call" | custom-call | tf_op jit(solution)/shard_map/muon_chain/pallas_call | solution.py:363
  150.8 17.7 %muon_pick.1 = f32[1,32,64,512]{3,2,1,0:T(8,128)} custom-call(s32[32]{0:T(128)} %select_reduce_fusion.index, s32[32]{0:T(128)} %convert_element_type.7.filled, bf16[64,64,512]{2,1,0:T(8,128)(2,1)} %muon_chain.1.in_ref), custom_call_target="tpu_custom_call" | custom-call | tf_op jit(solution)/shard_map/muon_pick/pallas_call | solution.py:400
  (1 shorter events, 0.0 us)
Async XLA Ops:
  2.9 1.6 copy-start

commit v3 on v2

--- a/solution.py
+++ b/solution.py
@@ -108,6 +108,7 @@
     columns = g_ref.shape[2]
     z, t = lax.axis_index("dp"), lax.axis_index("tensor")
     per_device = half // width
+    gap = half
     is_end = (z == 0) | (z == n - 1)
     low = 2 * z < n - 1
 
@@ -187,6 +188,13 @@
             device_id=(z + 1 - 2 * d, t),
             device_id_type=MESH,
         )
+
+    def pass_on(d, c):
+        ahead_copy(d, c).wait_recv()
+
+        @pl.when((z + 1 - 2 * d >= 0) & (z + 1 - 2 * d < n))
+        def _():
+            ahead_copy(d, c).start()
 
     def iterate_in(j):
         widened = whole[j].astype(jnp.float32) * (1.0 + decay_rate)
@@ -222,6 +230,13 @@
 
         lax.fori_loop(0, half, begin, 0)
 
+        def pass_group(j):
+            def one(k, inner):
+                pass_on(near, j * width + k)
+                return inner
+
+            lax.fori_loop(0, width, one, 0)
+
         def block_step(j, carry):
             def chunk(k, inner):
                 c = j * width + k
@@ -248,6 +263,11 @@
                 return inner
 
             lax.fori_loop(0, width, land, 0)
+
+            @pl.when(j > 0)
+            def _():
+                pass_group(j - 1)
+
             iterate_in(j)
 
             def give(k, inner):
@@ -268,6 +288,13 @@
             return carry
 
         lax.fori_loop(0, per_device, block_step, 0)
+        pass_group(per_device - 1)
+
+        def finish(c, carry):
+            pass_on(far, c)
+            return carry
+
+        lax.fori_loop(0, half, finish, 0)
 
     @pl.when(jnp.logical_not(is_end))
     def _():
@@ -282,36 +309,22 @@
             def _():
                 forward(early, i)
 
-            @pl.when(i >= lead)
+            @pl.when((i >= lead) & (i < half + lead))
             def _():
                 forward(1 - early, i - lead)
 
-            return carry
-
-        lax.fori_loop(0, half + lead, step, 0)
-
-    def pass_on(d, c):
-        ahead_copy(d, c).wait_recv()
-
-        @pl.when((z + 1 - 2 * d >= 0) & (z + 1 - 2 * d < n))
-        def _():
-            ahead_copy(d, c).start()
-
-    first = jnp.where(low, 0, 1)
-    delay = jnp.where(is_end, half, lead)
-
-    def gather_step(i, carry):
-        @pl.when(i < half)
-        def _():
-            pass_on(first, i)
-
-        @pl.when(i >= delay)
-        def _():
-            pass_on(1 - first, i - delay)
-
-        return carry
-
-    lax.fori_loop(0, half + delay, gather_step, 0)
+            @pl.when((i >= gap) & (i < half + gap))
+            def _():
+                pass_on(1 - early, i - gap)
+
+            @pl.when(i >= gap + lead)
+            def _():
+                pass_on(early, i - gap - lead)
+
+            return carry
+
+        lax.fori_loop(0, half + gap + lead, step, 0)
+
     final = pltpu.make_async_copy(gathered, out_ref, out_sem)
     final.start()
 
@@ -338,10 +351,11 @@
     final.wait()
 
 
-def pick_kernel(index, filled, in_ref, out_ref):
-    place = pl.program_id(0)
-    piece = in_ref[0].astype(jnp.float32)
-    out_ref[0, 0] = jnp.where(filled[place] > 0, piece, jnp.zeros_like(piece))
+def pick_kernel(group, index, filled, in_ref, out_ref):
+    base = pl.program_id(0) * group
+    for k in range(group):
+        piece = in_ref[index[base + k]].astype(jnp.float32)
+        out_ref[0, k] = jnp.where(filled[base + k] > 0, piece, jnp.zeros_like(piece))
 
 
 def fused(gradients, momentum, owners):
@@ -352,7 +366,7 @@
     blocks_all, rows, columns = pieces.shape
     capacity = momentum.shape[1]
     half = blocks_all // 2
-    lead = min(4, half)
+    lead = min(2, half)
     slot_rank = ranks_of(owners)
     mine = owners == me
     ratio = decay_rate * decay_rate / (1.0 + decay_rate)
@@ -397,14 +411,15 @@
     my_slots = mine[:, None] & (slot_rank[:, None] == slot_ids[None, :])
     filled = jnp.any(my_slots, axis=0).astype(jnp.int32)
     index = jnp.sum(jnp.where(my_slots, places[:, None], 0), axis=0)
+    group = math.gcd(capacity, 4)
     return pl.pallas_call(
-        pick_kernel,
+        functools.partial(pick_kernel, group),
         out_shape=jax.ShapeDtypeStruct((1, capacity, rows, columns), jnp.float32),
         grid_spec=pltpu.PrefetchScalarGridSpec(
             num_scalar_prefetch=2,
-            grid=(capacity,),
-            in_specs=[pl.BlockSpec((1, rows, columns), lambda s, index, filled: (index[s], 0, 0))],
-            out_specs=pl.BlockSpec((1, 1, rows, columns), lambda s, index, filled: (0, s, 0, 0)),
+            grid=(capacity // group,),
+            in_specs=[pl.BlockSpec(memory_space=pltpu.VMEM)],
+            out_specs=pl.BlockSpec((1, group, rows, columns), lambda s, index, filled: (0, s, 0, 0)),
         ),
         name="muon_pick",
     )(index, filled, all_results)

time: 170 us -> 127 us (0.75)
  the two profiles are of different devices: /device:TPU:28 before, /device:TPU:0 now
where the time goes in v3:
time: 127 us
  Pallas kernels  122 us (96%)
  other arithmetic  2.88 us (2%)
  local copies, waits for them, and re-layouts  1.59 us (1%)
    pallas_call x1, Pallas kernels, fused(): pl.pallas_call(functools.partial(kernel, (n, width, half, rows, lead)), o...  116 us
    pallas_call x1, Pallas kernels, fused(): pl.pallas_call(functools.partial(pick_kernel, group), out_shape=jax.Shape...  6.37 us

profile of v3, /device:TPU:0, one launch (start us, length us, event | category | flops | bytes accessed | tf_op | source)
XLA Modules:
  0.0 126.8 jit_solution(7554981375707770122)
XLA Ops:
  0.0 0.9 convert_reduce_fusion
  0.9 0.7 broadcast_select_fusion
  1.6 0.1 fusion.2
  1.7 0.6 select_reduce_fusion.index
  2.3 0.5 convert_element_type.7.filled
  2.9 0.0 copy-start
  2.9 1.6 %copy-done = bf16[1,32,64,512]{3,2,1,0:T(8,128)(2,1)S(1)} copy-done((bf16[1,32,64,512]{3,2,1,0:T(8,128)(2,1)S(1)}, bf16[1,32,64,512]{3,2,1,0:T(8,128)(2,1)}, u32[]{:S(2)}) %copy-start) | copy-done | bytes 2097176
  4.5 116.0 %muon_chain.1.in_ref = bf16[64,64,512]{2,1,0:T(8,128)(2,1)} custom-call(f32[64]{0:T(128)S(1)} %get-tuple-element.5.weight, s32[64]{0:T(128)S(1)} %broadcast_minimum_fusion.slot, bf16[64,64,512]{2,1,0:T(8,128)(2,1)} %bitcast.3, bf16[32,64,512]{2,1,0:T(8,128)(2,1)S(1)} %bitcast.2), custom_call_target="tpu_custom_call" | custom-call | tf_op jit(solution)/shard_map/muon_chain/pallas_call | solution.py:377
  120.5 6.4 %muon_pick.1 = f32[1,32,64,512]{3,2,1,0:T(8,128)} custom-call(s32[32]{0:T(128)} %select_reduce_fusion.index, s32[32]{0:T(128)} %convert_element_type.7.filled, bf16[64,64,512]{2,1,0:T(8,128)(2,1)} %muon_chain.1.in_ref), custom_call_target="tpu_custom_call" | custom-call | tf_op jit(solution)/shard_map/muon_pick/pallas_call | solution.py:415
  (1 shorter events, 0.0 us)
Async XLA Ops:
  2.9 1.6 %copy-start = (bf16[1,32,64,512]{3,2,1,0:T(8,128)(2,1)S(1)}, bf16[1,32,64,512]{3,2,1,0:T(8,128)(2,1)}, u32[]{:S(2)}) copy-start(bf16[1,32,64,512]{3,2,1,0:T(8,128)(2,1)} %param.4) | copy-start | bytes 6291460

commit v4 on v3

--- a/solution.py
+++ b/solution.py
@@ -237,7 +237,7 @@
 
             lax.fori_loop(0, width, one, 0)
 
-        def block_step(j, carry):
+        def reduce_group(j):
             def chunk(k, inner):
                 c = j * width + k
                 add_chain(near, c)
@@ -256,6 +256,7 @@
 
             lax.fori_loop(0, width, chunk, 0)
 
+        def iterate_group(j):
             def land(k, inner):
                 pltpu.make_async_copy(
                     partial.at[near, 0], whole.at[j, my_rows(k)], scatter_recv.at[j, k]
@@ -263,11 +264,6 @@
                 return inner
 
             lax.fori_loop(0, width, land, 0)
-
-            @pl.when(j > 0)
-            def _():
-                pass_group(j - 1)
-
             iterate_in(j)
 
             def give(k, inner):
@@ -285,9 +281,23 @@
                 return inner
 
             lax.fori_loop(0, width, give, 0)
-            return carry
-
-        lax.fori_loop(0, per_device, block_step, 0)
+
+        def block_step(j, carry):
+            @pl.when(j < per_device)
+            def _():
+                reduce_group(j)
+
+            @pl.when(j > 1)
+            def _():
+                pass_group(j - 2)
+
+            @pl.when(j > 0)
+            def _():
+                iterate_group(j - 1)
+
+            return carry
+
+        lax.fori_loop(0, per_device + 1, block_step, 0)
         pass_group(per_device - 1)
 
         def finish(c, carry):

time: 127 us -> 124 us (0.976)
  Pallas kernels: 122 us -> 119 us
    pallas_call x1, Pallas kernels: 116 us -> 113 us  [fused(): pl.pallas_call(functools.partial(kernel, (n, width, half, rows, lead)), o...]
where the time goes in v4:
time: 124 us; the launch traced here: 123 us
  Pallas kernels  119 us (96%)
  other arithmetic  2.88 us (2%)
  local copies, waits for them, and re-layouts  1.59 us (1%)
    pallas_call x1, Pallas kernels, fused(): pl.pallas_call(functools.partial(kernel, (n, width, half, rows, lead)), o...  113 us
    pallas_call x1, Pallas kernels, fused(): pl.pallas_call(functools.partial(pick_kernel, group), out_shape=jax.Shape...  6.37 us

profile of v4, /device:TPU:0, one launch (start us, length us, event | category | flops | bytes accessed | tf_op | source)
XLA Modules:
  0.0 123.4 jit_solution(4678419248059348578)
XLA Ops:
  0.0 0.9 convert_reduce_fusion
  0.9 0.7 broadcast_select_fusion
  1.6 0.1 fusion.2
  1.7 0.6 select_reduce_fusion.index
  2.3 0.5 convert_element_type.7.filled
  2.9 0.0 copy-start
  2.9 1.6 %copy-done = bf16[1,32,64,512]{3,2,1,0:T(8,128)(2,1)S(1)} copy-done((bf16[1,32,64,512]{3,2,1,0:T(8,128)(2,1)S(1)}, bf16[1,32,64,512]{3,2,1,0:T(8,128)(2,1)}, u32[]{:S(2)}) %copy-start) | copy-done | bytes 2097176
  4.5 112.6 %muon_chain.1.in_ref = bf16[64,64,512]{2,1,0:T(8,128)(2,1)} custom-call(f32[64]{0:T(128)S(1)} %get-tuple-element.5.weight, s32[64]{0:T(128)S(1)} %broadcast_minimum_fusion.slot, bf16[64,64,512]{2,1,0:T(8,128)(2,1)} %bitcast.3, bf16[32,64,512]{2,1,0:T(8,128)(2,1)S(1)} %bitcast.2), custom_call_target="tpu_custom_call" | custom-call | tf_op jit(solution)/shard_map/muon_chain/pallas_call | solution.py:387
  117.1 6.4 %muon_pick.1 = f32[1,32,64,512]{3,2,1,0:T(8,128)} custom-call(s32[32]{0:T(128)} %select_reduce_fusion.index, s32[32]{0:T(128)} %convert_element_type.7.filled, bf16[64,64,512]{2,1,0:T(8,128)(2,1)} %muon_chain.1.in_ref), custom_call_target="tpu_custom_call" | custom-call | tf_op jit(solution)/shard_map/muon_pick/pallas_call | solution.py:425
  (1 shorter events, 0.0 us)
Async XLA Ops:
  2.9 1.6 %copy-start = (bf16[1,32,64,512]{3,2,1,0:T(8,128)(2,1)S(1)}, bf16[1,32,64,512]{3,2,1,0:T(8,128)(2,1)}, u32[]{:S(2)}) copy-start(bf16[1,32,64,512]{3,2,1,0:T(8,128)(2,1)} %param.4) | copy-start | bytes 6291460
